TPU v7x, 32 devices: a whole 2x2x4 slice. The times are simulated.
32 devices in a mesh: groups: 2 (over y), wide: 16 (over z, x, core).
Axes of the slice: x: 2, y: 2, z: 4, core: 2. Of those that a mesh axis runs over, the one named last changes fastest.
Arguments:
- fields: bfloat16 [32, 512], P(('groups', 'wide')), parts along dimension 0, may hold values from -6 to 6
- chol: bfloat16 [512, 1024, 1024], P(None, 'wide'), may hold values from -0.01171875 to 0.01171875
- orbitals: bfloat16 [32, 1024, 256], P(('groups', 'wide')), parts along dimension 0, may hold values from -6 to 6
- trial: bfloat16 [1024, 256], replicated, may hold values from -0.5 to 0.5
Outputs:
- new_orbitals: bfloat16 [32, 1024, 256], P(('groups', 'wide')), parts along dimension 0
- force_bias: float32 [32, 2, 512], P(('groups', 'wide')), parts along dimension 0
There are 2 independent parts, one for each index of `groups`. A program takes and returns all parts, laid end to end along the dimension named above; an argument that names none is the same for every part. Nothing has to cross between parts.
All inputs are finite; a program needn't handle non-finite values.
Results may differ from a plain program's by a relative error of at most 0.0075.
Values may be sent and summed in bfloat16 or wider, within the bound.
No kernel may reach another device: no remote copies, remote signals or barrier semaphores. Data moves between devices by JAX's collectives and lax.ppermute only.
A program may use at most 192 MiB of HBM per device.

v0:
```python
import jax
import jax.numpy as jnp
from jax import lax
from jax.sharding import PartitionSpec as P

TAYLOR = 4


def per_device(fields, chol, orbitals, trial):
    all_fields = lax.all_gather(fields, "wide", axis=0, tiled=True)
    vectors, rows, width = chol.shape
    chol_flat = chol.reshape(vectors, rows * width)
    generator = jnp.dot(all_fields, chol_flat, preferred_element_type=jnp.float32).astype(
        jnp.bfloat16
    )
    generator = generator.reshape(all_fields.shape[0], rows, width)
    owned = lax.all_to_all(generator, "wide", split_axis=0, concat_axis=1, tiled=True)
    nocc = orbitals.shape[2] // 2
    walk_local = orbitals.shape[0]
    gen_walker = owned[0]
    total = orbitals[0].astype(jnp.float32)
    operand = orbitals[0]
    for order in range(1, TAYLOR + 1):
        product = jnp.dot(gen_walker, operand, preferred_element_type=jnp.float32)
        term = jnp.concatenate([-product[:, nocc:], product[:, :nocc]], axis=1) / order
        total = total + term
        if order < TAYLOR:
            operand = term.astype(jnp.bfloat16)
    fresh_list = [total.astype(jnp.bfloat16)]
    new_orbitals = jnp.stack(fresh_list, axis=0)
    trial_real = trial[:, :nocc].T
    trial_imag = trial[:, nocc:].T
    mixer = jnp.concatenate(
        [
            jnp.concatenate([trial_real, -trial_imag], axis=1),
            jnp.concatenate([trial_imag, trial_real], axis=1),
        ],
        axis=0,
    )
    orbital_rows = lax.all_to_all(new_orbitals, "wide", split_axis=1, concat_axis=0, tiled=True)
    count = orbital_rows.shape[0]
    flat_rows = orbital_rows.reshape(count * rows, 2 * nocc)
    tile_green = jnp.dot(flat_rows, mixer, preferred_element_type=jnp.float32).astype(jnp.bfloat16)
    tile_green = tile_green.reshape(count, rows, 2 * width)
    all_walk = tile_green.shape[0]
    tile_green = (
        tile_green.reshape(all_walk, rows, 2, width)
        .transpose(0, 2, 1, 3)
        .reshape(all_walk * 2, rows * width)
    )
    partial_value = jnp.dot(tile_green, chol_flat.T, preferred_element_type=jnp.float32).reshape(
        all_walk, 2, vectors
    )
    summed = lax.psum(partial_value, "wide")
    force_bias = lax.dynamic_slice_in_dim(
        summed, lax.axis_index("wide") * walk_local, walk_local, 0
    )
    return (new_orbitals, force_bias)


def solution(mesh):
    in_specs = (
        P(("groups", "wide"), None),
        P(None, "wide", None),
        P(("groups", "wide"), None, None),
        P(),
    )
    out_specs = (P(("groups", "wide"), None, None), P(("groups", "wide"), None, None))
    return jax.shard_map(
        per_device, mesh=mesh, in_specs=in_specs, out_specs=out_specs, check_vma=False
    )
```

profile of v0, /device:TPU:8, one launch (start us, length us, event | category | flops | bytes accessed | tf_op | source)
XLA Modules:
  0.0 381.3 jit_solution(17390543338026890626)
XLA Ops:
  7.2 58.5 %copy.31 = bf16[64,8,64,1024]{3,1,2,0:T(8,128)(2,1)} copy(bf16[64,8,64,1024]{3,2,1,0:T(8,128)(2,1)} %bitcast.19) | data formatting | bytes 134217728
  65.7 18.9 %all-gather = bf16[16,1,512]{2,1,0:T(2,128)(2,1)S(1)} all-gather(bf16[1,1,512]{2,1,0:T(2,128)(2,1)S(1)} %bitcast.65), channel_id=1, replica_groups=mesh['groups'=2,'wide'=16] {'wide'}, dimensions={0}, use_global_device_ids=true | all-gather | bytes 17408 | tf_op jit(solution)/shard_map/all_gather | solution.py:10
  84.6 22.8 %convolution_convert_fusion = bf16[16,65536]{1,0:T(8,128)(2,1)S(1)} fusion(bf16[512,65536]{1,0:T(8,128)(2,1)} %bitcast.20, bf16[16,1,512]{2,1,0:T(2,128)(2,1)S(1)} %all-gather), kind=kOutput, calls=%fused_computation | convolution fusion | flops 1074790400 | bytes 69222400 | tf_op jit(solution)/shard_map/dot_general | solution.py:13
  107.4 2.5 copy.32
  109.9 6.9 %all-to-all-start = ((bf16[16,64,1024]{2,1,0:T(8,128)(2,1)}), bf16[16,64,1024]{2,1,0:T(8,128)(2,1)S(1)}, u32[]{:S(2)}, u32[]{:S(2)}) async-start(bf16[16,64,1024]{2,1,0:T(8,128)(2,1)} %bitcast.62), calls=%async_computation | async-start | bytes 4194304 | tf_op jit(solution)/shard_map/all_to_all | solution.py:17
  116.8 0.2 copy.22
  117.0 45.6 %all-to-all-done = bf16[16,64,1024]{2,1,0:T(8,128)(2,1)S(1)} async-done(((bf16[16,64,1024]{2,1,0:T(8,128)(2,1)}), bf16[16,64,1024]{2,1,0:T(8,128)(2,1)S(1)}, u32[]{:S(2)}, u32[]{:S(2)}) %all-to-all-start) | async-done | bytes 2097184 | tf_op jit(solution)/shard_map/all_to_all | solution.py:17
  162.7 0.8 fusion.34
  163.4 0.1 fusion.38
  163.6 0.7 fusion.28
  164.3 0.1 slice_negate_fusion.2
  164.5 0.7 fusion.25
  165.2 0.1 slice_negate_fusion.1
  165.4 0.7 fusion.23
  166.1 0.1 fusion.27
  166.2 0.6 fusion.13
  166.8 0.9 copy.23
  167.7 0.5 broadcast.24
  168.2 3.8 %reduce = bf16[1024,256]{1,0:T(8,128)(2,1)S(1)} reduce(bf16[1024,1,256]{2,1,0:T(2,128)(2,1)S(1)} %bitcast.63, bf16[]{:T(256)} %broadcast.24), dimensions={1}, to_apply=%bitcast.50.reduce_sub_computation | reduce | bytes 1048578
  172.0 0.9 reshape.121
  172.9 6.4 %all-to-all-start.1 = ((bf16[16,2,8192]{2,1,0:T(2,128)(2,1)}), bf16[16,2,8192]{2,1,0:T(2,128)(2,1)S(1)}, u32[]{:S(2)}, u32[]{:S(2)}) async-start(bf16[16,2,8192]{2,1,0:T(2,128)(2,1)} %reshape.121), calls=%async_computation.1 | async-start | bytes 1048576 | tf_op jit(solution)/shard_map/all_to_all | solution.py:40
  179.3 0.0 all-reduce.2.cloned.1.call-start
  179.4 13.3 %all-to-all-done.1 = bf16[16,2,8192]{2,1,0:T(2,128)(2,1)S(1)} async-done(((bf16[16,2,8192]{2,1,0:T(2,128)(2,1)}), bf16[16,2,8192]{2,1,0:T(2,128)(2,1)S(1)}, u32[]{:S(2)}, u32[]{:S(2)}) %all-to-all-start.1) | async-done | bytes 524320 | tf_op jit(solution)/shard_map/all_to_all | solution.py:40
  192.8 0.5 reshape.122
  193.3 3.3 convolution_convert_fusion.1
  196.6 7.8 %reshape_reshape.3 = bf16[16,64,2,1024]{3,2,1,0:T(2,128)(2,1)} reshape(bf16[1024,2048]{1,0:T(8,128)(2,1)} %convolution_convert_fusion.1) | data formatting | bytes 8388608 | tf_op jit(solution)/shard_map/reshape;reshape | solution.py:47
  204.3 80.0 %fusion.5 = f32[16,2,512]{2,0,1:T(8,128)} fusion(bf16[512,64,1024]{2,1,0:T(8,128)(2,1)} %param.5, bf16[16,64,2,1024]{3,2,1,0:T(2,128)(2,1)} %reshape_reshape.3), kind=kOutput, calls=%fused_computation.7 | convolution fusion | flops 2147483648 | bytes 71368704 | tf_op jit(solution)/shard_map/dot_general | solution.py:51
  284.3 0.0 all-reduce.2.cloned.1.call-update
  284.3 1.0 copy.26
  285.3 87.8 %all-reduce.2.cloned.1.call-done = f32[16,2,512]{2,0,1:T(8,128)} async-done(((f32[16,2,512]{2,0,1:T(8,128)}), f32[16,2,512]{2,0,1:T(8,128)}) %all-reduce.2.cloned.1.call-update) | async-done | bytes 65552 | tf_op jit(solution)/shard_map/psum | solution.py:54
  373.1 0.8 constant_dynamic-slice_fusion
  373.9 0.6 copy.27
  (9 shorter events, 0.1 us)
Async XLA Ops:
  7.2 58.6 %copy-start.2 = (bf16[1,512]{1,0:T(2,128)(2,1)S(1)}, bf16[1,512]{1,0:T(2,128)(2,1)}, u32[]{:S(2)}) copy-start(bf16[1,512]{1,0:T(2,128)(2,1)} %param.4) | copy-start | bytes 3076
  109.9 6.9 %copy-start = (bf16[1,1024,256]{2,1,0:T(8,128)(2,1)S(1)}, bf16[1,1024,256]{2,1,0:T(8,128)(2,1)}, u32[]{:S(2)}) copy-start(bf16[1,1024,256]{2,1,0:T(8,128)(2,1)} %param.6) | copy-start | bytes 1572868
  109.9 52.8 %all-to-all-start = ((bf16[16,64,1024]{2,1,0:T(8,128)(2,1)}), bf16[16,64,1024]{2,1,0:T(8,128)(2,1)S(1)}, u32[]{:S(2)}, u32[]{:S(2)}) async-start(bf16[16,64,1024]{2,1,0:T(8,128)(2,1)} %bitcast.62), calls=%async_computation | async-start | bytes 4194304 | tf_op jit(solution)/shard_map/all_to_all | solution.py:17
  167.6 11.7 %copy-start.1 = (bf16[1024,256]{1,0:T(8,128)(2,1)S(1)}, bf16[1024,256]{1,0:T(8,128)(2,1)}, u32[]{:S(2)}) copy-start(bf16[1024,256]{1,0:T(8,128)(2,1)} %param.7) | copy-start | bytes 1572868
  172.9 19.8 %all-to-all-start.1 = ((bf16[16,2,8192]{2,1,0:T(2,128)(2,1)}), bf16[16,2,8192]{2,1,0:T(2,128)(2,1)S(1)}, u32[]{:S(2)}, u32[]{:S(2)}) async-start(bf16[16,2,8192]{2,1,0:T(2,128)(2,1)} %reshape.121), calls=%async_computation.1 | async-start | bytes 1048576 | tf_op jit(solution)/shard_map/all_to_all | solution.py:40
  179.3 193.8 %all-reduce.2.cloned.1.call-start = ((), (), s32[]{:S(2)}) async-start(), calls=%async_computation.2 | async-start | bytes 131072 | tf_op jit(solution)/shard_map/psum | solution.py:54
Sparse Core Ops, SparseCore 0:
  284.4 88.6 all-reduce.1
where the time goes:
time: 382 us; the launch traced here: 381 us
  waiting for transfers between devices  147 us (38%)
  matrix products  109 us (29%)
  local copies, waits for them, and re-layouts  74.3 us (19%)
  blocking collectives  18.9 us (5%)
  between operations  14.2 us (4%)
  starting transfers between devices  13.3 us (3%)
  other arithmetic  4.9 us (1%)
    psum x1, waiting for transfers between devices, per_device(): summed = lax.psum(partial_value, 'wide')  87.8 us
    dot_general x1, matrix products, per_device(): jnp.dot(tile_green, chol_flat.T, preferred_element_type=jnp.float32)  80 us
    unnamed x14, local copies, waits for them, and re-layouts  64.8 us
    all_to_all x1, waiting for transfers between devices, per_device(): lax.all_to_all(generator, 'wide', split_axis=0, concat_axis=1, tiled=True)  45.6 us
    dot_general x1, matrix products, per_device(): jnp.dot(all_fields, chol_flat, preferred_element_type=jnp.float32)  22.8 us
    all_gather x1, blocking collectives, per_device(): all_fields = lax.all_gather(fields, 'wide', axis=0, tiled=True)  18.9 us
    all_to_all x1, waiting for transfers between devices, per_device(): lax.all_to_all(new_orbitals, 'wide', split_axis=1, concat_axis=0, tiled=T...  13.3 us
    another operation x1, local copies, waits for them, and re-layouts, per_device(): tile_green.reshape(all_walk, rows, 2, width).transpose(0, 2, 1, 3)  7.78 us
  transfers between devices with their start and end apart: 3, of which 3 were waited for; matrix products, arithmetic and copies ran while one was open for 0% of the time, Pallas kernels for 0%

commit v1 on v0

--- a/solution.py
+++ b/solution.py
@@ -14,7 +14,12 @@
         jnp.bfloat16
     )
     generator = generator.reshape(all_fields.shape[0], rows, width)
-    owned = lax.all_to_all(generator, "wide", split_axis=0, concat_axis=1, tiled=True)
+    owned = jnp.concatenate(
+        lax.all_to_all(
+            jnp.stack(jnp.split(generator, lax.axis_size("wide"), axis=0)), "wide", 0, 0
+        ),
+        axis=1,
+    )
     nocc = orbitals.shape[2] // 2
     walk_local = orbitals.shape[0]
     gen_walker = owned[0]

time: 382 us -> 410 us (1.073)
  local copies, waits for them, and re-layouts: 74.3 us -> 103 us
    split x0 -> x1, local copies, waits for them, and re-layouts: none -> 15 us  [per_device(): jnp.split(generator, lax.axis_size('wide'), axis=0)]
    unnamed x14 -> x28, local copies, waits for them, and re-layouts: 64.8 us -> 72.1 us
    another operation x0 -> x17, local copies, waits for them, and re-layouts: none -> 6.15 us  [per_device(): jnp.stack(jnp.split(generator, lax.axis_size('wide'), axis=0))]
where the time goes in v1:
time: 410 us
  waiting for transfers between devices  147 us (36%)
  matrix products  109 us (27%)
  local copies, waits for them, and re-layouts  103 us (25%)
  blocking collectives  18.9 us (5%)
  between operations  14.3 us (3%)
  starting transfers between devices  13.3 us (3%)
  other arithmetic  4.9 us (1%)
    psum x1, waiting for transfers between devices, per_device(): summed = lax.psum(partial_value, 'wide')  87.7 us
    dot_general x1, matrix products, per_device(): jnp.dot(tile_green, chol_flat.T, preferred_element_type=jnp.float32)  80 us
    unnamed x28, local copies, waits for them, and re-layouts  72.1 us
    all_to_all x1, waiting for transfers between devices, per_device(): lax.all_to_all(jnp.stack(jnp.split(generator, lax.axis_size('wide'), axis...  45.6 us
    dot_general x1, matrix products, per_device(): jnp.dot(all_fields, chol_flat, preferred_element_type=jnp.float32)  22.8 us
    all_gather x1, blocking collectives, per_device(): all_fields = lax.all_gather(fields, 'wide', axis=0, tiled=True)  18.9 us
    split x1, local copies, waits for them, and re-layouts, per_device(): jnp.split(generator, lax.axis_size('wide'), axis=0)  15 us
    all_to_all x1, waiting for transfers between devices, per_device(): lax.all_to_all(new_orbitals, 'wide', split_axis=1, concat_axis=0, tiled=T...  13.3 us
  transfers between devices with their start and end apart: 3, of which 3 were waited for; matrix products, arithmetic and copies ran while one was open for 0% of the time, Pallas kernels for 0%

profile of v1, /device:TPU:8, one launch (start us, length us, event | category | flops | bytes accessed | tf_op | source)
XLA Modules:
  0.0 409.9 jit_solution(10497610426979989556)
XLA Ops:
  7.2 58.5 %copy.31 = bf16[64,8,64,1024]{3,1,2,0:T(8,128)(2,1)} copy(bf16[64,8,64,1024]{3,2,1,0:T(8,128)(2,1)} %bitcast.19) | data formatting | bytes 134217728
  65.7 18.9 %all-gather = bf16[16,1,512]{2,1,0:T(2,128)(2,1)S(1)} all-gather(bf16[1,1,512]{2,1,0:T(2,128)(2,1)S(1)} %bitcast.61), channel_id=1, replica_groups=mesh['groups'=2,'wide'=16] {'wide'}, dimensions={0}, use_global_device_ids=true | all-gather | bytes 17408 | tf_op jit(solution)/shard_map/all_gather | solution.py:10
  84.6 22.8 %convolution_convert_fusion = bf16[16,65536]{1,0:T(8,128)(2,1)S(1)} fusion(bf16[512,65536]{1,0:T(8,128)(2,1)} %bitcast.20, bf16[16,1,512]{2,1,0:T(2,128)(2,1)S(1)} %all-gather), kind=kOutput, calls=%fused_computation | convolution fusion | flops 1074790400 | bytes 69222400 | tf_op jit(solution)/shard_map/dot_general | solution.py:13
  107.4 15.0 %slice_reduce_fusion = (bf16[65536]{0:T(1024)(128)(2,1)S(1)}, bf16[65536]{0:T(1024)(128)(2,1)S(1)}, bf16[65536]{0:T(1024)(128)(2,1)S(1)}, bf16[65536]{0:T(1024)(...) fusion(bf16[16,65536]{1,0:T(8,128)(2,1)S(1)} %convolution_conve, ...), kind=kLoop, calls=%fused_computation.49 | loop fusion | bytes 4194304 | tf_op jit(solution)/shard_map/split | solution.py:19
  122.3 1.0 stack.52
  124.0 1.0 stack.53
  124.9 1.0 stack.54
  125.9 1.0 stack.55
  126.9 1.0 stack.56
  128.6 0.7 constant_dynamic-update-slice_fusion.14
  129.2 0.7 constant_dynamic-update-slice_fusion.13
  132.5 0.7 constant_dynamic-update-slice_fusion.8
  133.9 0.7 constant_dynamic-update-slice_fusion.6
  135.2 0.7 constant_dynamic-update-slice_fusion.4
  137.8 0.7 constant_dynamic-update-slice_fusion
  138.5 6.9 %all-to-all-start = ((bf16[16,1,64,1024]{3,2,1,0:T(8,128)(2,1)}), bf16[16,1,64,1024]{3,2,1,0:T(8,128)(2,1)S(1)}, u32[]{:S(2)}, u32[]{:S(2)}) async-start(bf16[16,1,64,1024]{3,2,1,0:T(8,128)(2,1)} %constant_dynamic-update-slice_fusion), calls=%async_computation | async-start | bytes 4194304 | tf_op jit(solution)/shard_map/all_to_all | solution.py:18
  145.6 45.6 %all-to-all-done = bf16[16,1,64,1024]{3,2,1,0:T(8,128)(2,1)S(1)} async-done(((bf16[16,1,64,1024]{3,2,1,0:T(8,128)(2,1)}), bf16[16,1,64,1024]{3,2,1,0:T(8,128)(2,1)S(1)}, u32[]{:S(2)}, u32[]{:S(2)}) %all-to-all-start) | async-done | bytes 2097184 | tf_op jit(solution)/shard_map/all_to_all | solution.py:18
  191.2 0.8 fusion.34
  192.2 0.7 fusion.28
  193.1 0.7 fusion.25
  194.0 0.7 fusion.23
  195.4 0.9 copy.23
  196.7 3.8 reduce.32
  200.6 0.9 reshape.162
  201.5 6.4 %all-to-all-start.1 = ((bf16[16,2,8192]{2,1,0:T(2,128)(2,1)}), bf16[16,2,8192]{2,1,0:T(2,128)(2,1)S(1)}, u32[]{:S(2)}, u32[]{:S(2)}) async-start(bf16[16,2,8192]{2,1,0:T(2,128)(2,1)} %reshape.162), calls=%async_computation.1 | async-start | bytes 1048576 | tf_op jit(solution)/shard_map/all_to_all | solution.py:45
  208.0 13.3 %all-to-all-done.1 = bf16[16,2,8192]{2,1,0:T(2,128)(2,1)S(1)} async-done(((bf16[16,2,8192]{2,1,0:T(2,128)(2,1)}), bf16[16,2,8192]{2,1,0:T(2,128)(2,1)S(1)}, u32[]{:S(2)}, u32[]{:S(2)}) %all-to-all-start.1) | async-done | bytes 524320 | tf_op jit(solution)/shard_map/all_to_all | solution.py:45
  221.9 3.3 convolution_convert_fusion.1
  225.1 7.8 %reshape_reshape.3 = bf16[16,64,2,1024]{3,2,1,0:T(2,128)(2,1)} reshape(bf16[1024,2048]{1,0:T(8,128)(2,1)} %convolution_convert_fusion.1) | data formatting | bytes 8388608 | tf_op jit(solution)/shard_map/reshape;reshape | solution.py:52
  232.9 80.0 %fusion.5 = f32[16,2,512]{2,0,1:T(8,128)} fusion(bf16[512,64,1024]{2,1,0:T(8,128)(2,1)} %param.5, bf16[16,64,2,1024]{3,2,1,0:T(2,128)(2,1)} %reshape_reshape.3), kind=kOutput, calls=%fused_computation.7 | convolution fusion | flops 2147483648 | bytes 71368704 | tf_op jit(solution)/shard_map/dot_general | solution.py:56
  312.9 1.0 copy.26
  313.9 87.7 %all-reduce.2.cloned.1.call-done = f32[16,2,512]{2,0,1:T(8,128)} async-done(((f32[16,2,512]{2,0,1:T(8,128)}), f32[16,2,512]{2,0,1:T(8,128)}) %all-reduce.2.cloned.1.call-update) | async-done | bytes 65552 | tf_op jit(solution)/shard_map/psum | solution.py:59
  401.7 0.8 constant_dynamic-slice_fusion
  (41 shorter events, 10.3 us)
Async XLA Ops:
  7.2 58.5 %copy-start.2 = (bf16[1,512]{1,0:T(2,128)(2,1)S(1)}, bf16[1,512]{1,0:T(2,128)(2,1)}, u32[]{:S(2)}) copy-start(bf16[1,512]{1,0:T(2,128)(2,1)} %param.4) | copy-start | bytes 3076
  138.5 6.9 %copy-start = (bf16[1,1024,256]{2,1,0:T(8,128)(2,1)S(1)}, bf16[1,1024,256]{2,1,0:T(8,128)(2,1)}, u32[]{:S(2)}) copy-start(bf16[1,1024,256]{2,1,0:T(8,128)(2,1)} %param.6) | copy-start | bytes 1572868
  138.5 52.8 %all-to-all-start = ((bf16[16,1,64,1024]{3,2,1,0:T(8,128)(2,1)}), bf16[16,1,64,1024]{3,2,1,0:T(8,128)(2,1)S(1)}, u32[]{:S(2)}, u32[]{:S(2)}) async-start(bf16[16,1,64,1024]{3,2,1,0:T(8,128)(2,1)} %constant_dynamic-update-slice_fusion), calls=%async_computation | async-start | bytes 4194304 | tf_op jit(solution)/shard_map/all_to_all | solution.py:18
  196.2 11.7 %copy-start.1 = (bf16[1024,256]{1,0:T(8,128)(2,1)S(1)}, bf16[1024,256]{1,0:T(8,128)(2,1)}, u32[]{:S(2)}) copy-start(bf16[1024,256]{1,0:T(8,128)(2,1)} %param.7) | copy-start | bytes 1572868
  201.5 19.8 %all-to-all-start.1 = ((bf16[16,2,8192]{2,1,0:T(2,128)(2,1)}), bf16[16,2,8192]{2,1,0:T(2,128)(2,1)S(1)}, u32[]{:S(2)}, u32[]{:S(2)}) async-start(bf16[16,2,8192]{2,1,0:T(2,128)(2,1)} %reshape.162), calls=%async_computation.1 | async-start | bytes 1048576 | tf_op jit(solution)/shard_map/all_to_all | solution.py:45
  207.8 193.8 %all-reduce.2.cloned.1.call-start = ((), (), s32[]{:S(2)}) async-start(), calls=%async_computation.2 | async-start | bytes 131072 | tf_op jit(solution)/shard_map/psum | solution.py:59
Sparse Core Ops, SparseCore 0:
  313.1 88.5 all-reduce.1
